TPU v7x, 256 devices: a whole 4x4x8 slice. The times are simulated.
256 devices in a mesh: grid: 16 (over y, x), mic: 4 (over z_hi), bin: 4 (over z_lo, core).
Axes of the slice: x: 4, y: 4, z: 8 (z_hi: 4, z_lo: 2; z = z_hi * 2 + z_lo), core: 2. Of those that a mesh axis runs over, the one named last changes fastest.
Arguments:
- grid_points: float32 [3, 16384], P(None, 'grid'), may hold values from -1 to 3, as said below
- mic_coords: float32 [3, 4096], P(None, 'mic'), may hold values from -1 to 1, as said below
- wavenumbers: float32 [16], P('bin'), may hold values from 20 to 150
- pressures: float32 [16, 2, 16, 4096], P('bin', None, None, 'mic'), may hold values from -6 to 6
Outputs:
- solution: float32 [16, 2, 16, 16384], P('bin', None, None, 'grid')
- residual: float32 [16, 2, 16, 4096], P('bin', None, None, 'mic')
Inputs may be any that keep to these rules, and one draw needn't show every extreme that they name: `grid_points`: rows 0 and 1 lie in -1 to 1, row 2 in 1 to 3. `mic_coords`: rows 0 and 1 lie in -1 to 1, row 2 in -0.05 to 0.05.
All inputs are finite; a program needn't handle non-finite values.
Results may differ from a plain program's by a relative error of at most 0.0055.
Values may be sent and summed in bfloat16 or wider, within the bound.
No kernel may reach another device: no remote copies, remote signals or barrier semaphores. Data moves between devices by JAX's collectives and lax.ppermute only.
A program may use at most 64 MiB of HBM per device.

v0:
```python
import math
import jax
import jax.numpy as jnp
from jax import lax
from jax.sharding import PartitionSpec as P

ITERS = 2


def steering_tiles(grid_points, mic_coords, wavenumbers, norm_scale):
    dist_x = grid_points[0][:, None] - mic_coords[0][None, :]
    dist_y = grid_points[1][:, None] - mic_coords[1][None, :]
    dist_z = grid_points[2][:, None] - mic_coords[2][None, :]
    radius = jnp.sqrt(dist_x * dist_x + dist_y * dist_y + dist_z * dist_z)
    amplitude = norm_scale / radius
    cos_list = []
    sin_list = []
    for bin_index in range(wavenumbers.shape[0]):
        phase_angle = wavenumbers[bin_index] * radius
        cos_list.append((jnp.cos(phase_angle) * amplitude).astype(jnp.bfloat16))
        sin_list.append((jnp.sin(phase_angle) * amplitude).astype(jnp.bfloat16))
    return (jnp.stack(cos_list), jnp.stack(sin_list))


def body(grid_points, mic_coords, wavenumbers, pressures):
    bin_count = pressures.shape[0]
    snap_count = pressures.shape[2]
    grid_local = grid_points.shape[1]
    norm_scale = 1.0 / math.sqrt(grid_local * lax.axis_size("grid"))
    cos_tiles, sin_tiles = steering_tiles(grid_points, mic_coords, wavenumbers, norm_scale)

    def combine_adjoint(cos_sum, sin_sum):
        real_part = cos_sum[:, :snap_count] - sin_sum[:, snap_count:]
        imag_part = cos_sum[:, snap_count:] + sin_sum[:, :snap_count]
        return jnp.stack([real_part, imag_part], axis=1)

    def apply_adjoint(residual):
        rounded = residual.astype(jnp.bfloat16).reshape(
            bin_count, 2 * snap_count, residual.shape[3]
        )
        cos_sum = jnp.einsum("fkm,fgm->fkg", rounded, cos_tiles, preferred_element_type=jnp.float32)
        sin_sum = jnp.einsum("fkm,fgm->fkg", rounded, sin_tiles, preferred_element_type=jnp.float32)
        partial_terms = combine_adjoint(cos_sum, sin_sum)
        summed = lax.psum(partial_terms, "mic")
        grad_norm = lax.psum(jnp.sum(summed * summed), ("grid", "bin"))
        return (summed, grad_norm)

    residual = pressures
    gradient, grad_norm = apply_adjoint(residual)
    direction = gradient
    solution = jnp.zeros_like(gradient)
    for iteration in range(ITERS):
        apply_rounded = direction.astype(jnp.bfloat16).reshape(
            bin_count, 2 * snap_count, direction.shape[3]
        )
        apply_cos_sum = jnp.einsum(
            "fkg,fgm->fkm", apply_rounded, cos_tiles, preferred_element_type=jnp.float32
        )
        apply_sin_sum = jnp.einsum(
            "fkg,fgm->fkm", apply_rounded, sin_tiles, preferred_element_type=jnp.float32
        )
        combine_real_part = apply_cos_sum[:, :snap_count] + apply_sin_sum[:, snap_count:]
        combine_imag_part = apply_cos_sum[:, snap_count:] - apply_sin_sum[:, :snap_count]
        apply_partial_terms = jnp.stack([combine_real_part, combine_imag_part], axis=1)
        apply_summed = lax.psum(apply_partial_terms, "grid")
        image_norm = lax.psum(jnp.sum(apply_summed * apply_summed), ("mic", "bin"))
        image, image_norm = (apply_summed, image_norm)
        step_size = grad_norm / image_norm
        solution = solution + step_size * direction
        residual = residual - step_size * image
        if iteration + 1 < ITERS:
            gradient, next_norm = apply_adjoint(residual)
            direction = gradient + next_norm / grad_norm * direction
            grad_norm = next_norm
    return (solution, residual)


def solution(mesh):
    placed = (P(None, "grid"), P(None, "mic"), P("bin"), P("bin", None, None, "mic"))
    return jax.shard_map(
        body,
        mesh=mesh,
        in_specs=placed,
        out_specs=(P("bin", None, None, "grid"), P("bin", None, None, "mic")),
        check_vma=False,
    )
```

profile of v0, /device:TPU:1, one launch (start us, length us, event | category | flops | bytes accessed | tf_op | source)
XLA Modules:
  0.0 768.9 jit_solution(6533060130410521625)
XLA Ops:
  7.2 1.5 fusion.13
  8.7 0.8 fusion.11
  9.5 0.8 fusion.12
  10.4 1.1 convert_element_type.96
  11.5 67.4 %multiply_convert_fusion.7 = (bf16[1,1024,1024]{2,1,0:T(8,128)(2,1)S(1)}, bf16[1,1024,1024]{2,1,0:T(8,128)(2,1)S(1)}, bf16[1,1024,1024]{2,1,0:T(8,128)(2,1)S(1)}...) fusion(f32[1024]{0:T(1024)S(1)} %bitcast.62, ...), kind=kLoop, calls=%fused_computation.9 | loop fusion | flops 30408704 | bytes 16801808 | tf_op jit(solution)/shard_map/convert_element_type | solution.py:20
  78.9 2.4 pad_maximum_fusion
  81.3 2.6 convolution_bitcast_fusion
  84.5 2.5 copy-done.2
  87.0 2.6 convolution_bitcast_fusion.1
  89.6 0.8 pad_maximum_fusion.2
  90.6 56.2 %all-reduce.5.cloned.1.call-done = f32[4,2,16,1024]{3,2,0,1:T(8,128)} async-done(((f32[4,2,16,1024]{3,2,0,1:T(8,128)}), f32[4,2,16,1024]{3,2,0,1:T(8,128)}) %all-reduce.5.cloned.1.call-update) | async-done | bytes 524304 | tf_op jit(solution)/shard_map/psum | solution.py:44
  146.7 1.9 multiply_reduce_fusion.3
  148.7 5.1 fusion.14
  154.5 1.5 fusion.15
  156.1 0.8 pad_maximum_fusion.3
  157.0 94.4 %all-reduce.7.cloned.1.call-done = f32[4,2,16,1024]{3,2,0,1:T(8,128)} async-done(((f32[4,2,16,1024]{3,2,0,1:T(8,128)}), f32[4,2,16,1024]{3,2,0,1:T(8,128)}) %all-reduce.7.cloned.1.call-update) | async-done | bytes 524304 | tf_op jit(solution)/shard_map/psum | solution.py:65
  251.4 1.8 multiply_reduce_fusion.2
  253.2 140.4 %psum.57 = f32[]{:T(128)} all-reduce(f32[]{:T(128)} %get-tuple-element.14), channel_id=1, replica_groups=mesh['grid'=16,'mic'=4,'bin'=4] {'grid','bin'}, use_global_device_ids=true, to_apply=%region_2.0 | all-reduce | flops 1 | bytes 8 | tf_op jit(solution)/shard_map/psum | solution.py:45
  393.6 25.9 %psum.59 = f32[]{:T(128)} all-reduce(f32[]{:T(128)} %multiply_reduce_fusion.2), channel_id=1, replica_groups=mesh['grid'=16,'mic'=4,'bin'=4] {'mic','bin'}, use_global_device_ids=true, to_apply=%region_5.0 | all-reduce | flops 1 | bytes 8 | tf_op jit(solution)/shard_map/psum | solution.py:66
  420.8 1.1 fusion.10
  422.0 5.9 fusion.16
  427.9 6.0 fusion.17
  434.9 47.9 %all-reduce.9.cloned.1.call-done = f32[4,2,16,1024]{3,2,0,1:T(8,128)} async-done(((f32[4,2,16,1024]{3,2,0,1:T(8,128)}), f32[4,2,16,1024]{3,2,0,1:T(8,128)}) %all-reduce.9.cloned.1.call-update) | async-done | bytes 524304 | tf_op jit(solution)/shard_map/psum | solution.py:44
  482.8 1.8 multiply_reduce_fusion.1
  484.6 140.7 %psum.61 = f32[]{:T(128)} all-reduce(f32[]{:T(128)} %multiply_reduce_fusion.1), channel_id=1, replica_groups=mesh['grid'=16,'mic'=4,'bin'=4] {'grid','bin'}, use_global_device_ids=true, to_apply=%region_8.0 | all-reduce | flops 1 | bytes 8 | tf_op jit(solution)/shard_map/psum | solution.py:45
  626.6 1.1 fusion.9
  627.8 4.9 fusion.18
  632.7 5.0 fusion.19
  638.6 91.7 %all-reduce.11.cloned.1.call-done = f32[4,2,16,1024]{3,2,0,1:T(8,128)} async-done(((f32[4,2,16,1024]{3,2,0,1:T(8,128)}), f32[4,2,16,1024]{3,2,0,1:T(8,128)}) %all-reduce.11.cloned.1.call-update) | async-done | bytes 524304 | tf_op jit(solution)/shard_map/psum | solution.py:65
  730.4 1.8 multiply_reduce_fusion
  732.1 26.0 %psum.63 = f32[]{:T(128)} all-reduce(f32[]{:T(128)} %multiply_reduce_fusion), channel_id=1, replica_groups=mesh['grid'=16,'mic'=4,'bin'=4] {'mic','bin'}, use_global_device_ids=true, to_apply=%region_11.0 | all-reduce | flops 1 | bytes 8 | tf_op jit(solution)/shard_map/psum | solution.py:66
  759.4 1.2 multiply_subtract_fusion
  (33 shorter events, 5.3 us)
Async XLA Ops:
  7.2 139.6 %all-reduce.5.cloned.1.call-start = ((), (), s32[]{:S(2)}) async-start(), calls=%async_computation | async-start | bytes 1048576 | tf_op jit(solution)/shard_map/psum | solution.py:44
  81.3 3.2 copy-start
  81.3 5.7 copy-start.2
  90.5 160.9 %all-reduce.7.cloned.1.call-start = ((), (), s32[]{:S(2)}) async-start(), calls=%async_computation.1 | async-start | bytes 1048576 | tf_op jit(solution)/shard_map/psum | solution.py:65
  148.7 5.8 copy-start.1
  154.5 266.4 %copy-start.5 = (f32[4,2,16,1024]{3,2,1,0:T(8,128)S(1)}, f32[4,2,16,1024]{3,2,1,0:T(8,128)}, u32[]{:S(2)}) copy-start(f32[4,2,16,1024]{3,2,1,0:T(8,128)} %param.7) | copy-start | bytes 1572868
  156.9 325.9 %all-reduce.9.cloned.1.call-start = ((), (), s32[]{:S(2)}) async-start(), calls=%async_computation.2 | async-start | bytes 1048576 | tf_op jit(solution)/shard_map/psum | solution.py:44
  427.9 198.7 %copy-start.3 = (f32[4,2,16,1024]{3,2,0,1:T(8,128)S(1)}, f32[4,2,16,1024]{3,2,0,1:T(8,128)}, u32[]{:S(2)}) copy-start(f32[4,2,16,1024]{3,2,0,1:T(8,128)} %all-reduce.5.cloned.1.call-done) | copy-start | bytes 1572868
  434.9 295.5 %all-reduce.11.cloned.1.call-start = ((), (), s32[]{:S(2)}) async-start(), calls=%async_computation.3 | async-start | bytes 1048576 | tf_op jit(solution)/shard_map/psum | solution.py:65
  632.7 126.7 %copy-start.6 = (f32[4,2,16,1024]{3,2,0,1:T(8,128)S(1)}, f32[4,2,16,1024]{3,2,0,1:T(8,128)}, u32[]{:S(2)}) copy-start(f32[4,2,16,1024]{3,2,0,1:T(8,128)} %all-reduce.7.cloned.1.call-done) | copy-start | bytes 1572868
  637.7 123.8 %copy-start.4 = (f32[4,2,16,1024]{3,2,0,1:T(8,128)S(1)}, f32[4,2,16,1024]{3,2,0,1:T(8,128)}, u32[]{:S(2)}) copy-start(f32[4,2,16,1024]{3,2,0,1:T(8,128)} %all-reduce.9.cloned.1.call-done) | copy-start | bytes 1572868
Sparse Core Ops, SparseCore 0:
  90.6 56.0 all-reduce.4
  157.1 94.3 all-reduce.6
  435.0 47.7 all-reduce.8
  638.7 91.5 all-reduce.10
where the time goes:
time: 770 us; the launch traced here: 769 us
  blocking collectives  333 us (43%)
  waiting for transfers between devices  290 us (38%)
  other arithmetic  85.2 us (11%)
  matrix products  33.6 us (4%)
  between operations  17.9 us (2%)
  local copies, waits for them, and re-layouts  8.73 us (1%)
    psum x2, blocking collectives, apply_adjoint(): grad_norm = lax.psum(jnp.sum(summed * summed), ('grid', 'bin'))  281 us
    psum x2, waiting for transfers between devices, body(): apply_summed = lax.psum(apply_partial_terms, 'grid')  186 us
    psum x2, waiting for transfers between devices, apply_adjoint(): summed = lax.psum(partial_terms, 'mic')  104 us
    convert_element_type x1, other arithmetic, steering_tiles(): cos_list.append((jnp.cos(phase_angle) * amplitude).astype(jnp.bfloat16))  67.4 us
    psum x2, blocking collectives, body(): image_norm = lax.psum(jnp.sum(apply_summed * apply_summed), ('mic', 'bin'))  51.9 us
  transfers between devices with their start and end apart: 4, of which 4 were waited for; matrix products, arithmetic and copies ran while one was open for 0% of the time, Pallas kernels for 0%

commit v1 on v0

--- a/solution.py
+++ b/solution.py
@@ -62,7 +62,10 @@
         combine_real_part = apply_cos_sum[:, :snap_count] + apply_sin_sum[:, snap_count:]
         combine_imag_part = apply_cos_sum[:, snap_count:] - apply_sin_sum[:, :snap_count]
         apply_partial_terms = jnp.stack([combine_real_part, combine_imag_part], axis=1)
-        apply_summed = lax.psum(apply_partial_terms, "grid")
+        count, apply_summed = (lax.axis_size("grid"), apply_partial_terms)
+        for far in [1 << k for k in range(count.bit_length() - 1)]:
+            swap = [(i, i ^ far) for i in range(count)]
+            apply_summed = apply_summed + lax.ppermute(apply_summed, "grid", swap)
         image_norm = lax.psum(jnp.sum(apply_summed * apply_summed), ("mic", "bin"))
         image, image_norm = (apply_summed, image_norm)
         step_size = grad_norm / image_norm

time: 770 us -> 664 us (0.86)
  waiting for transfers between devices: 290 us -> 165 us
  starting transfers between devices: 0.16 us -> 15.4 us
  blocking collectives: 333 us -> 341 us
    psum x2 -> x0, waiting for transfers between devices: 186 us -> none  [body(): apply_summed = lax.psum(apply_partial_terms, 'grid')]
    ppermute x0 -> x8, waiting for transfers between devices: none -> 62.8 us  [body(): apply_summed = apply_summed + lax.ppermute(apply_summed, 'grid', swap)]
    ppermute x0 -> x8, starting transfers between devices: none -> 15.3 us  [body(): apply_summed = apply_summed + lax.ppermute(apply_summed, 'grid', swap)]
  transfers between devices with their start and end apart: 4 -> 10, of which waited for: 4 -> 9; matrix products, arithmetic and copies ran while one was open for 0% -> 0% of each run, Pallas kernels for 0% -> 0%
where the time goes in v1:
time: 664 us; the launch traced here: 662 us
  blocking collectives  341 us (51%)
  waiting for transfers between devices  165 us (25%)
  other arithmetic  80.1 us (12%)
  matrix products  33.5 us (5%)
  between operations  18.3 us (3%)
  starting transfers between devices  15.4 us (2%)
  local copies, waits for them, and re-layouts  8.73 us (1%)
    psum x2, blocking collectives, apply_adjoint(): grad_norm = lax.psum(jnp.sum(summed * summed), ('grid', 'bin'))  284 us
    psum x2, waiting for transfers between devices, apply_adjoint(): summed = lax.psum(partial_terms, 'mic')  102 us
    convert_element_type x1, other arithmetic, steering_tiles(): cos_list.append((jnp.cos(phase_angle) * amplitude).astype(jnp.bfloat16))  67.5 us
    ppermute x8, waiting for transfers between devices, body(): apply_summed = apply_summed + lax.ppermute(apply_summed, 'grid', swap)  62.8 us
    psum x2, blocking collectives, body(): image_norm = lax.psum(jnp.sum(apply_summed * apply_summed), ('mic', 'bin'))  56.9 us
    ppermute x8, starting transfers between devices, body(): apply_summed = apply_summed + lax.ppermute(apply_summed, 'grid', swap)  15.3 us
  transfers between devices with their start and end apart: 10, of which 9 were waited for; matrix products, arithmetic and copies ran while one was open for 0% of the time, Pallas kernels for 0%

profile of v1, /device:TPU:1, one launch (start us, length us, event | category | flops | bytes accessed | tf_op | source)
XLA Modules:
  0.0 662.4 jit_solution(17077937740760529066)
XLA Ops:
  7.2 1.5 fusion.15
  11.4 67.5 %multiply_convert_fusion.7 = (bf16[1,1024,1024]{2,1,0:T(8,128)(2,1)S(1)}, bf16[1,1024,1024]{2,1,0:T(8,128)(2,1)S(1)}, bf16[1,1024,1024]{2,1,0:T(8,128)(2,1)S(1)}...) fusion(f32[1024]{0:T(1024)S(1)} %bitcast.62, ...), kind=kLoop, calls=%fused_computation.9 | loop fusion | flops 30408704 | bytes 16801808 | tf_op jit(solution)/shard_map/convert_element_type | solution.py:20
  78.9 2.4 pad_maximum_fusion
  81.3 2.6 convolution_bitcast_fusion
  84.5 2.5 copy-done.2
  87.0 2.6 convolution_bitcast_fusion.1
  90.6 56.0 %all-reduce.3.cloned.1.call-done = f32[4,2,16,1024]{3,2,0,1:T(8,128)} async-done(((f32[4,2,16,1024]{3,2,0,1:T(8,128)}), f32[4,2,16,1024]{3,2,0,1:T(8,128)}) %all-reduce.3.cloned.1.call-update) | async-done | bytes 524304 | tf_op jit(solution)/shard_map/psum | solution.py:44
  146.6 1.9 multiply_reduce_fusion.3
  148.6 5.1 fusion.16
  154.3 1.5 fusion.17
  156.0 1.4 collective-permute-start
  157.4 9.9 %collective-permute-done = f32[4,2,16,1024]{3,2,0,1:T(8,128)S(1)} collective-permute-done((f32[4,2,16,1024]{3,2,0,1:T(8,128)S(1)}, f32[4,2,16,1024]{3,2,0,1:T(8,128)S(1)}, u32[]{:S(2)}, u32[]{:S(2)}) %collective-permute-start) | collective-permute-done | bytes 524320 | tf_op jit(solution)/shard_map/ppermute | solution.py:68
  167.4 2.9 collective-permute-start.1
  170.3 10.1 %collective-permute-done.1 = f32[4,2,16,1024]{3,2,0,1:T(8,128)S(1)} collective-permute-done((f32[4,2,16,1024]{3,2,0,1:T(8,128)S(1)}, f32[4,2,16,1024]{3,2,0,1:T(8,128)S(1)}, u32[]{:S(2)}, u32[]{:S(2)}) %collective-permute-start.1) | collective-permute-done | bytes 524320 | tf_op jit(solution)/shard_map/ppermute | solution.py:68
  180.6 1.2 collective-permute-start.2
  181.7 8.9 %collective-permute-done.2 = f32[4,2,16,1024]{3,2,0,1:T(8,128)S(1)} collective-permute-done((f32[4,2,16,1024]{3,2,0,1:T(8,128)S(1)}, f32[4,2,16,1024]{3,2,0,1:T(8,128)S(1)}, u32[]{:S(2)}, u32[]{:S(2)}) %collective-permute-start.2) | collective-permute-done | bytes 524320 | tf_op jit(solution)/shard_map/ppermute | solution.py:68
  190.7 2.6 collective-permute-start.3
  193.3 143.7 %psum.43 = f32[]{:T(128)} all-reduce(f32[]{:T(128)} %get-tuple-element.18), channel_id=1, replica_groups=mesh['grid'=16,'mic'=4,'bin'=4] {'grid','bin'}, use_global_device_ids=true, to_apply=%region_2.0 | all-reduce | flops 1 | bytes 8 | tf_op jit(solution)/shard_map/psum | solution.py:45
  337.8 24.2 %psum.44 = f32[]{:T(128)} all-reduce(f32[]{:T(128)} %get-tuple-element.8), channel_id=1, replica_groups=mesh['grid'=16,'mic'=4,'bin'=4] {'mic','bin'}, use_global_device_ids=true, to_apply=%region_4.0 | all-reduce | flops 1 | bytes 8 | tf_op jit(solution)/shard_map/psum | solution.py:69
  363.5 5.9 fusion.18
  369.5 6.0 fusion.19
  376.4 46.2 %all-reduce.5.cloned.1.call-done = f32[4,2,16,1024]{3,2,0,1:T(8,128)} async-done(((f32[4,2,16,1024]{3,2,0,1:T(8,128)}), f32[4,2,16,1024]{3,2,0,1:T(8,128)}) %all-reduce.5.cloned.1.call-update) | async-done | bytes 524304 | tf_op jit(solution)/shard_map/psum | solution.py:44
  422.7 1.8 multiply_reduce_fusion.1
  424.4 140.6 %psum.46 = f32[]{:T(128)} all-reduce(f32[]{:T(128)} %multiply_reduce_fusion.1), channel_id=1, replica_groups=mesh['grid'=16,'mic'=4,'bin'=4] {'grid','bin'}, use_global_device_ids=true, to_apply=%region_7.0 | all-reduce | flops 1 | bytes 8 | tf_op jit(solution)/shard_map/psum | solution.py:45
  567.5 4.9 fusion.20
  572.5 4.9 fusion.21
  577.6 8.6 %collective-permute-done.4 = f32[4,2,16,1024]{3,2,0,1:T(8,128)S(1)} collective-permute-done((f32[4,2,16,1024]{3,2,0,1:T(8,128)S(1)}, f32[4,2,16,1024]{3,2,0,1:T(8,128)S(1)}, u32[]{:S(2)}, u32[]{:S(2)}) %collective-permute-start.4) | collective-permute-done | bytes 524320 | tf_op jit(solution)/shard_map/ppermute | solution.py:68
  586.4 9.5 %collective-permute-done.5 = f32[4,2,16,1024]{3,2,0,1:T(8,128)S(1)} collective-permute-done((f32[4,2,16,1024]{3,2,0,1:T(8,128)S(1)}, f32[4,2,16,1024]{3,2,0,1:T(8,128)S(1)}, u32[]{:S(2)}, u32[]{:S(2)}) %collective-permute-start.5) | collective-permute-done | bytes 524320 | tf_op jit(solution)/shard_map/ppermute | solution.py:68
  596.1 8.3 %collective-permute-done.6 = f32[4,2,16,1024]{3,2,0,1:T(8,128)S(1)} collective-permute-done((f32[4,2,16,1024]{3,2,0,1:T(8,128)S(1)}, f32[4,2,16,1024]{3,2,0,1:T(8,128)S(1)}, u32[]{:S(2)}, u32[]{:S(2)}) %collective-permute-start.6) | collective-permute-done | bytes 524320 | tf_op jit(solution)/shard_map/ppermute | solution.py:68
  604.5 6.9 %collective-permute-start.7 = (f32[4,2,16,1024]{3,2,0,1:T(8,128)S(1)}, f32[4,2,16,1024]{3,2,0,1:T(8,128)S(1)}, u32[]{:S(2)}, u32[]{:S(2)}) collective-permute-start(f32[4,2,16,1024]{3,2,0,1:T(8,128)S(1)} %add.143), channel_id=1, source_target_pairs={{0,128},{16,144},{32,160},{48,176},{64,192},{80,208},{96,224},{112... | collective-permute-start | bytes 1572872 | tf_op jit(solution)/shard_map/ppermute | solution.py:68
  611.4 7.4 %collective-permute-done.7 = f32[4,2,16,1024]{3,2,0,1:T(8,128)S(1)} collective-permute-done((f32[4,2,16,1024]{3,2,0,1:T(8,128)S(1)}, f32[4,2,16,1024]{3,2,0,1:T(8,128)S(1)}, u32[]{:S(2)}, u32[]{:S(2)}) %collective-permute-start.7) | collective-permute-done | bytes 524320 | tf_op jit(solution)/shard_map/ppermute | solution.py:68
  619.6 32.7 %psum.47 = f32[]{:T(128)} all-reduce(f32[]{:T(128)} %get-tuple-element.6), channel_id=1, replica_groups=mesh['grid'=16,'mic'=4,'bin'=4] {'mic','bin'}, use_global_device_ids=true, to_apply=%region_9.0 | all-reduce | flops 1 | bytes 8 | tf_op jit(solution)/shard_map/psum | solution.py:69
  (47 shorter events, 11.7 us)
Async XLA Ops:
  7.2 139.4 %all-reduce.3.cloned.1.call-start = ((), (), s32[]{:S(2)}) async-start(), calls=%async_computation | async-start | bytes 1048576 | tf_op jit(solution)/shard_map/psum | solution.py:44
  81.3 3.2 copy-start
  81.3 5.7 copy-start.2
  90.5 332.1 %all-reduce.5.cloned.1.call-start = ((), (), s32[]{:S(2)}) async-start(), calls=%async_computation.1 | async-start | bytes 1048576 | tf_op jit(solution)/shard_map/psum | solution.py:44
  148.6 5.8 copy-start.1
  156.0 207.4 %copy-start.5 = (f32[4,2,16,1024]{3,2,1,0:T(8,128)S(1)}, f32[4,2,16,1024]{3,2,1,0:T(8,128)}, u32[]{:S(2)}) copy-start(f32[4,2,16,1024]{3,2,1,0:T(8,128)} %param.7) | copy-start | bytes 1572868
  156.0 11.3 %collective-permute-start = (f32[4,2,16,1024]{3,2,0,1:T(8,128)S(1)}, f32[4,2,16,1024]{3,2,0,1:T(8,128)S(1)}, u32[]{:S(2)}, u32[]{:S(2)}) collective-permute-start(f32[4,2,16,1024]{3,2,0,1:T(8,128)S(1)} %pad_maximum_fusion.3), channel_id=1, source_target_pairs={{0,16},{16,0},{32,48},{48,32},{64,80},{80,64},{96,112},{112,96},{1... | collective-permute-start | bytes 1572872 | tf_op jit(solution)/shard_map/ppermute | solution.py:68
  167.4 13.1 %collective-permute-start.1 = (f32[4,2,16,1024]{3,2,0,1:T(8,128)S(1)}, f32[4,2,16,1024]{3,2,0,1:T(8,128)S(1)}, u32[]{:S(2)}, u32[]{:S(2)}) collective-permute-start(f32[4,2,16,1024]{3,2,0,1:T(8,128)S(1)} %fusion.12), channel_id=1, source_target_pairs={{0,32},{16,48},{32,0},{48,16},{64,96},{80,112},{96,64},{112,80},{1... | collective-permute-start | bytes 1572872 | tf_op jit(solution)/shard_map/ppermute | solution.py:68
  180.6 10.1 %collective-permute-start.2 = (f32[4,2,16,1024]{3,2,0,1:T(8,128)S(1)}, f32[4,2,16,1024]{3,2,0,1:T(8,128)S(1)}, u32[]{:S(2)}, u32[]{:S(2)}) collective-permute-start(f32[4,2,16,1024]{3,2,0,1:T(8,128)S(1)} %fusion.39), channel_id=1, source_target_pairs={{0,64},{16,80},{32,96},{48,112},{64,0},{80,16},{96,32},{112,48},{1... | collective-permute-start | bytes 1572872 | tf_op jit(solution)/shard_map/ppermute | solution.py:68
  190.7 146.3 %collective-permute-start.3 = (f32[4,2,16,1024]{3,2,0,1:T(8,128)S(1)}, f32[4,2,16,1024]{3,2,0,1:T(8,128)S(1)}, u32[]{:S(2)}, u32[]{:S(2)}) collective-permute-start(f32[4,2,16,1024]{3,2,0,1:T(8,128)S(1)} %add.136), channel_id=1, source_target_pairs={{0,128},{16,144},{32,160},{48,176},{64,192},{80,208},{96,224},{112... | collective-permute-start | bytes 1572872 | tf_op jit(solution)/shard_map/ppermute | solution.py:68
  369.5 196.9 %copy-start.3 = (f32[4,2,16,1024]{3,2,0,1:T(8,128)S(1)}, f32[4,2,16,1024]{3,2,0,1:T(8,128)}, u32[]{:S(2)}) copy-start(f32[4,2,16,1024]{3,2,0,1:T(8,128)} %all-reduce.3.cloned.1.call-done) | copy-start | bytes 1572868
  577.5 8.7 %collective-permute-start.4 = (f32[4,2,16,1024]{3,2,0,1:T(8,128)S(1)}, f32[4,2,16,1024]{3,2,0,1:T(8,128)S(1)}, u32[]{:S(2)}, u32[]{:S(2)}) collective-permute-start(f32[4,2,16,1024]{3,2,0,1:T(8,128)S(1)} %pad_maximum_fusion.5), channel_id=1, source_target_pairs={{0,16},{16,0},{32,48},{48,32},{64,80},{80,64},{96,112},{112,96},{1... | collective-permute-start | bytes 1572872 | tf_op jit(solution)/shard_map/ppermute | solution.py:68
  586.3 68.3 %copy-start.4 = (f32[4,2,16,1024]{3,2,0,1:T(8,128)S(1)}, f32[4,2,16,1024]{3,2,0,1:T(8,128)}, u32[]{:S(2)}) copy-start(f32[4,2,16,1024]{3,2,0,1:T(8,128)} %all-reduce.5.cloned.1.call-done) | copy-start | bytes 1572868
  586.3 9.6 %collective-permute-start.5 = (f32[4,2,16,1024]{3,2,0,1:T(8,128)S(1)}, f32[4,2,16,1024]{3,2,0,1:T(8,128)S(1)}, u32[]{:S(2)}, u32[]{:S(2)}) collective-permute-start(f32[4,2,16,1024]{3,2,0,1:T(8,128)S(1)} %fusion.11), channel_id=1, source_target_pairs={{0,32},{16,48},{32,0},{48,16},{64,96},{80,112},{96,64},{112,80},{1... | collective-permute-start | bytes 1572872 | tf_op jit(solution)/shard_map/ppermute | solution.py:68
  596.0 8.4 %collective-permute-start.6 = (f32[4,2,16,1024]{3,2,0,1:T(8,128)S(1)}, f32[4,2,16,1024]{3,2,0,1:T(8,128)S(1)}, u32[]{:S(2)}, u32[]{:S(2)}) collective-permute-start(f32[4,2,16,1024]{3,2,0,1:T(8,128)S(1)} %fusion.38), channel_id=1, source_target_pairs={{0,64},{16,80},{32,96},{48,112},{64,0},{80,16},{96,32},{112,48},{1... | collective-permute-start | bytes 1572872 | tf_op jit(solution)/shard_map/ppermute | solution.py:68
  604.5 14.3 %collective-permute-start.7 = (f32[4,2,16,1024]{3,2,0,1:T(8,128)S(1)}, f32[4,2,16,1024]{3,2,0,1:T(8,128)S(1)}, u32[]{:S(2)}, u32[]{:S(2)}) collective-permute-start(f32[4,2,16,1024]{3,2,0,1:T(8,128)S(1)} %add.143), channel_id=1, source_target_pairs={{0,128},{16,144},{32,160},{48,176},{64,192},{80,208},{96,224},{112... | collective-permute-start | bytes 1572872 | tf_op jit(solution)/shard_map/ppermute | solution.py:68
Sparse Core Ops, SparseCore 0:
  90.6 55.9 all-reduce.2
  376.5 46.0 all-reduce.4
